TPU v7x, 32 devices: a whole 2x2x4 slice. The times are simulated.
32 devices in a mesh: group: 2 (over y), col: 4 (over z), row: 2 (over x), section: 2 (over core).
Axes of the slice: x: 2, y: 2, z: 4, core: 2. Of those that a mesh axis runs over, the one named last changes fastest.
Arguments:
- tokens: bfloat16 [2, 256, 8192], P(None, ('group', 'col'), 'row'), parts along dimension 1, may hold values from -12 to 12, as said below
- norm_gain: float32 [2, 8192], P('section', 'row'), may hold values from 0.5 to 1.5
- w_gate: bfloat16 [2, 8192, 14336], P('section', 'row', 'col'), may hold values from -0.0625 to 0.0625
- w_up: bfloat16 [2, 8192, 14336], P('section', 'row', 'col'), may hold values from -0.0625 to 0.0625
- w_down: bfloat16 [2, 14336, 8192], P('section', 'col', 'row'), may hold values from -0.046875 to 0.046875
Outputs:
- block_out: bfloat16 [2, 2, 256, 8192], P('section', None, ('group', 'col'), 'row'), parts along dimension 2
There are 2 independent parts, one for each index of `group`. A program takes and returns all parts, laid end to end along the dimension named above; an argument that names none is the same for every part. Nothing has to cross between parts.
Inputs may be any that keep to these rules, and one draw needn't show every extreme that they name: `tokens`: dense real activations.
All inputs are finite; a program needn't handle non-finite values.
Results may differ from a plain program's by a relative error of at most 0.024.
Values may be sent and summed in bfloat16 or wider, within the bound.
A program may use at most 128 MiB of HBM per device.

v0:
```python
import jax
import jax.numpy as jnp
from jax import lax
from jax.sharding import PartitionSpec as P

D = 8192
EPS = 1e-05


def from_behind(value, axis, steps):
    count = lax.axis_size(axis)
    initial, last = (max(0, -steps), min(count, count - steps))
    return lax.ppermute(value, axis, [(source, source + steps) for source in range(initial, last)])


def on_device(tokens, norm_gain, w_gate, w_up, w_down):
    section_index = lax.axis_index("section")
    is_first = section_index == 0
    gain = norm_gain[0]
    gate_tile = w_gate[0]
    up_tile = w_up[0]
    down_tile = w_down[0]
    micro, tok_col, width_row = tokens.shape
    hidden_cols = gate_tile.shape[1]
    results = []
    received = jnp.zeros((tok_col, width_row), jnp.bfloat16)
    for tick in range(micro + 1):
        fresh = tokens[tick] if tick < micro else jnp.zeros((tok_col, width_row), jnp.bfloat16)
        block_in = jnp.where(is_first, fresh, received)
        wide_in = block_in.astype(jnp.float32)
        sum_sq = lax.psum(jnp.sum(wide_in * wide_in, axis=1), "row")
        wide = block_in.astype(jnp.float32)
        scale = lax.rsqrt(sum_sq / D + EPS)
        normed = (wide * scale[:, None] * gain[None, :]).astype(jnp.bfloat16)
        normed_rows = lax.all_gather(normed, "col", axis=0, tiled=True)
        gate_part = jnp.dot(normed_rows, gate_tile, preferred_element_type=jnp.float32)
        up_part = jnp.dot(normed_rows, up_tile, preferred_element_type=jnp.float32)
        pair = jnp.concatenate([gate_part, up_part], axis=1)
        share = lax.psum_scatter(
            pair.astype(jnp.bfloat16), "row", scatter_dimension=0, tiled=True
        ).astype(jnp.float32)
        hidden_share = (jax.nn.silu(share[:, :hidden_cols]) * share[:, hidden_cols:]).astype(
            jnp.bfloat16
        )
        hidden = lax.all_gather(hidden_share, "row", axis=0, tiled=True)
        ffn = lax.psum_scatter(
            jnp.dot(hidden, down_tile, preferred_element_type=jnp.float32).astype(jnp.bfloat16),
            "col",
            scatter_dimension=0,
            tiled=True,
        ).astype(jnp.float32)
        result = (wide_in + ffn).astype(jnp.bfloat16)
        results.append(result)
        if tick < micro:
            received = from_behind(result, "section", 1)
    early = jnp.stack(results[:micro], axis=0)
    late = jnp.stack(results[1:], axis=0)
    return jnp.where(is_first, early, late)[None]


def solution(mesh):
    placed = (
        P(None, ("group", "col"), "row"),
        P("section", "row"),
        P("section", "row", "col"),
        P("section", "row", "col"),
        P("section", "col", "row"),
    )
    return jax.shard_map(
        on_device,
        mesh=mesh,
        in_specs=placed,
        out_specs=P("section", None, ("group", "col"), "row"),
        check_vma=False,
    )
```

profile of v0, /device:TPU:0, one launch (start us, length us, event | category | flops | bytes accessed | tf_op | source)
XLA Modules:
  0.0 455.9 jit_solution(14409287867418705781)
XLA Ops:
  6.5 1.1 fusion.56
  7.7 5.9 %psum.21 = f32[32]{0:T(128)S(1)} all-reduce(f32[32]{0:T(128)S(1)} %fusion.56), channel_id=1, replica_groups=mesh['group'=2,'col'=4,'row'=2,'section'=2] {'row'}, use_global_device_ids=true, to_apply=%region_1.2 | all-reduce | flops 32 | bytes 256 | tf_op jit(solution)/shard_map/psum | solution.py:31
  13.5 1.8 fusion.58
  15.4 29.9 %all-gather.4.cloned.1.call-done = bf16[128,4096]{1,0:T(8,128)(2,1)} async-done(((bf16[32,4096]{1,0:T(8,128)(2,1)}), bf16[128,4096]{1,0:T(8,128)(2,1)}) %all-gather.4.cloned.1.call-update) | async-done | bytes 1048592 | tf_op jit(solution)/shard_map/all_gather | solution.py:35
  45.3 13.7 %fusion.27 = bf16[128,3584]{1,0:T(8,128)(2,1)S(1)} fusion(bf16[128,4096]{1,0:T(8,128)(2,1)} %all-gather.4.cloned.1.call-done, bf16[1,4096,3584]{2,1,0:T(8,128)(2,1)} %param.8), kind=kOutput, calls=%fused_computation.21 | convolution fusion | flops 3758555136 | bytes 31326208 | tf_op jit(solution)/shard_map/dot_general | solution.py:37
  59.0 11.6 %fusion.18 = bf16[128,3584]{1,0:T(8,128)(2,1)S(1)} fusion(bf16[128,4096]{1,0:T(8,128)(2,1)S(1)} %copy-done, bf16[1,4096,3584]{2,1,0:T(8,128)(2,1)} %param.7), kind=kOutput, calls=%fused_computation.18 | convolution fusion | flops 3758555136 | bytes 31326208 | tf_op jit(solution)/shard_map/dot_general | solution.py:36
  70.6 1.4 pad_maximum_fusion
  72.1 28.5 %reduce-scatter.7.cloned.1.call-done = bf16[64,7168]{1,0:T(8,128)(2,1)} async-done(((bf16[128,7168]{1,0:T(8,128)(2,1)}), bf16[64,7168]{1,0:T(8,128)(2,1)}) %reduce-scatter.7.cloned.1.call-update) | async-done | bytes 917520 | tf_op jit(solution)/shard_map/reduce_scatter | solution.py:39
  100.6 1.3 convert_element_type.75
  101.9 0.2 fusion.47
  102.2 12.8 %all_gather.19 = bf16[128,3584]{1,0:T(8,128)(2,1)S(1)} all-gather(bf16[64,3584]{1,0:T(8,128)(2,1)S(1)} %fusion.47), channel_id=1, replica_groups=mesh['group'=2,'col'=4,'row'=2,'section'=2] {'row'}, dimensions={0}, use_global_device_ids=true | all-gather | bytes 1376256 | tf_op jit(solution)/shard_map/all_gather | solution.py:45
  115.0 12.6 %fusion.36 = bf16[128,4096]{1,0:T(8,128)(2,1)} fusion(bf16[128,3584]{1,0:T(8,128)(2,1)S(1)} %all_gather.19, bf16[1,3584,4096]{2,1,0:T(8,128)(2,1)} %param.9), kind=kOutput, calls=%fused_computation.24 | convolution fusion | flops 3758620672 | bytes 31326208 | tf_op jit(solution)/shard_map/dot_general | solution.py:47
  127.6 27.4 %reduce-scatter.9.cloned.1.call-done = bf16[32,4096]{1,0:T(8,128)(2,1)} async-done(((bf16[128,4096]{1,0:T(8,128)(2,1)}), bf16[32,4096]{1,0:T(8,128)(2,1)}) %reduce-scatter.9.cloned.1.call-update) | async-done | bytes 262160 | tf_op jit(solution)/shard_map/reduce_scatter | solution.py:46
  155.1 1.0 fusion.59
  156.1 1.3 collective-permute-start
  157.4 1.1 collective-permute-done
  158.6 0.2 fusion.48
  158.8 4.9 %psum.22 = f32[32]{0:T(128)S(1)} all-reduce(f32[32]{0:T(128)S(1)} %get-tuple-element.5), channel_id=1, replica_groups=mesh['group'=2,'col'=4,'row'=2,'section'=2] {'row'}, use_global_device_ids=true, to_apply=%region_5.6 | all-reduce | flops 32 | bytes 256 | tf_op jit(solution)/shard_map/psum | solution.py:31
  163.7 0.8 fusion.50
  164.6 0.2 reduce-scatter.11.cloned.1.call-start
  164.8 26.8 %all-gather.6.cloned.1.call-done = bf16[128,4096]{1,0:T(8,128)(2,1)} async-done(((bf16[32,4096]{1,0:T(8,128)(2,1)}), bf16[128,4096]{1,0:T(8,128)(2,1)}) %all-gather.6.cloned.1.call-update) | async-done | bytes 1048592 | tf_op jit(solution)/shard_map/all_gather | solution.py:35
  191.6 13.7 %fusion.30 = bf16[128,3584]{1,0:T(8,128)(2,1)S(1)} fusion(bf16[128,4096]{1,0:T(8,128)(2,1)} %all-gather.6.cloned.1.call-done, bf16[1,4096,3584]{2,1,0:T(8,128)(2,1)} %param.8), kind=kOutput, calls=%fused_computation.22 | convolution fusion | flops 3758555136 | bytes 31326208 | tf_op jit(solution)/shard_map/dot_general | solution.py:37
  205.3 11.6 %fusion.21 = bf16[128,3584]{1,0:T(8,128)(2,1)S(1)} fusion(bf16[128,4096]{1,0:T(8,128)(2,1)S(1)} %copy-done.1, bf16[1,4096,3584]{2,1,0:T(8,128)(2,1)} %param.7), kind=kOutput, calls=%fused_computation.19 | convolution fusion | flops 3758555136 | bytes 31326208 | tf_op jit(solution)/shard_map/dot_general | solution.py:36
  216.9 1.4 pad_maximum_fusion.1
  218.4 28.5 %reduce-scatter.11.cloned.1.call-done = bf16[64,7168]{1,0:T(8,128)(2,1)} async-done(((bf16[128,7168]{1,0:T(8,128)(2,1)}), bf16[64,7168]{1,0:T(8,128)(2,1)}) %reduce-scatter.11.cloned.1.call-update) | async-done | bytes 917520 | tf_op jit(solution)/shard_map/reduce_scatter | solution.py:39
  246.9 1.3 convert_element_type.82
  248.2 0.2 fusion.46
  248.5 12.8 %all_gather.21 = bf16[128,3584]{1,0:T(8,128)(2,1)S(1)} all-gather(bf16[64,3584]{1,0:T(8,128)(2,1)S(1)} %fusion.46), channel_id=1, replica_groups=mesh['group'=2,'col'=4,'row'=2,'section'=2] {'row'}, dimensions={0}, use_global_device_ids=true | all-gather | bytes 1376256 | tf_op jit(solution)/shard_map/all_gather | solution.py:45
  261.2 12.5 %fusion.39 = bf16[128,4096]{1,0:T(8,128)(2,1)} fusion(bf16[128,3584]{1,0:T(8,128)(2,1)S(1)} %all_gather.21, bf16[1,3584,4096]{2,1,0:T(8,128)(2,1)} %param.9), kind=kOutput, calls=%fused_computation.25 | convolution fusion | flops 3758620672 | bytes 31326208 | tf_op jit(solution)/shard_map/dot_general | solution.py:47
  273.8 27.4 %reduce-scatter.13.cloned.1.call-done = bf16[32,4096]{1,0:T(8,128)(2,1)} async-done(((bf16[128,4096]{1,0:T(8,128)(2,1)}), bf16[32,4096]{1,0:T(8,128)(2,1)}) %reduce-scatter.13.cloned.1.call-update) | async-done | bytes 262160 | tf_op jit(solution)/shard_map/reduce_scatter | solution.py:46
  301.3 1.0 fusion.51
  302.3 1.3 collective-permute-start.1
  303.6 1.1 collective-permute-done.1
  304.9 4.9 %psum.23 = f32[32]{0:T(128)S(1)} all-reduce(f32[32]{0:T(128)S(1)} %fusion.52), channel_id=1, replica_groups=mesh['group'=2,'col'=4,'row'=2,'section'=2] {'row'}, use_global_device_ids=true, to_apply=%region_9.10 | all-reduce | flops 32 | bytes 256 | tf_op jit(solution)/shard_map/psum | solution.py:31
  309.9 0.8 fusion.54
  310.7 0.3 reduce-scatter.15.cloned.1.call-start
  311.0 26.7 %all-gather.8.cloned.1.call-done = bf16[128,4096]{1,0:T(8,128)(2,1)} async-done(((bf16[32,4096]{1,0:T(8,128)(2,1)}), bf16[128,4096]{1,0:T(8,128)(2,1)}) %all-gather.8.cloned.1.call-update) | async-done | bytes 1048592 | tf_op jit(solution)/shard_map/all_gather | solution.py:35
  337.7 13.7 %fusion.33 = bf16[128,3584]{1,0:T(8,128)(2,1)S(1)} fusion(bf16[128,4096]{1,0:T(8,128)(2,1)} %all-gather.8.cloned.1.call-done, bf16[1,4096,3584]{2,1,0:T(8,128)(2,1)} %param.8), kind=kOutput, calls=%fused_computation.23 | convolution fusion | flops 3758555136 | bytes 31326208 | tf_op jit(solution)/shard_map/dot_general | solution.py:37
  351.5 11.6 %fusion.24 = bf16[128,3584]{1,0:T(8,128)(2,1)S(1)} fusion(bf16[128,4096]{1,0:T(8,128)(2,1)S(1)} %copy-done.2, bf16[1,4096,3584]{2,1,0:T(8,128)(2,1)} %param.7), kind=kOutput, calls=%fused_computation.20 | convolution fusion | flops 3758555136 | bytes 31326208 | tf_op jit(solution)/shard_map/dot_general | solution.py:36
  363.1 1.4 pad_maximum_fusion.2
  364.6 28.5 %reduce-scatter.15.cloned.1.call-done = bf16[64,7168]{1,0:T(8,128)(2,1)} async-done(((bf16[128,7168]{1,0:T(8,128)(2,1)}), bf16[64,7168]{1,0:T(8,128)(2,1)}) %reduce-scatter.15.cloned.1.call-update) | async-done | bytes 917520 | tf_op jit(solution)/shard_map/reduce_scatter | solution.py:39
  393.1 1.3 convert_element_type.89
  394.4 0.2 fusion.45
  394.6 12.8 %all_gather.23 = bf16[128,3584]{1,0:T(8,128)(2,1)S(1)} all-gather(bf16[64,3584]{1,0:T(8,128)(2,1)S(1)} %fusion.45), channel_id=1, replica_groups=mesh['group'=2,'col'=4,'row'=2,'section'=2] {'row'}, dimensions={0}, use_global_device_ids=true | all-gather | bytes 1376256 | tf_op jit(solution)/shard_map/all_gather | solution.py:45
  407.4 12.5 %fusion.42 = bf16[128,4096]{1,0:T(8,128)(2,1)} fusion(bf16[128,3584]{1,0:T(8,128)(2,1)S(1)} %all_gather.23, bf16[1,3584,4096]{2,1,0:T(8,128)(2,1)} %param.9), kind=kOutput, calls=%fused_computation.26 | convolution fusion | flops 3758620672 | bytes 31326208 | tf_op jit(solution)/shard_map/dot_general | solution.py:47
  419.9 27.5 %reduce-scatter.17.cloned.1.call-done = bf16[32,4096]{1,0:T(8,128)(2,1)} async-done(((bf16[128,4096]{1,0:T(8,128)(2,1)}), bf16[32,4096]{1,0:T(8,128)(2,1)}) %reduce-scatter.17.cloned.1.call-update) | async-done | bytes 262160 | tf_op jit(solution)/shard_map/reduce_scatter | solution.py:46
  447.4 1.0 fusion.60
  448.4 0.9 maximum_select_fusion
  (30 shorter events, 0.6 us)
Async XLA Ops:
  6.5 38.8 %all-gather.4.cloned.1.call-start = ((), (), s32[]{:S(2)}) async-start(), calls=%async_computation.6 | async-start | bytes 1310720 | tf_op jit(solution)/shard_map/all_gather | solution.py:35
  15.4 85.3 %reduce-scatter.7.cloned.1.call-start = ((), (), s32[]{:S(2)}) async-start(), calls=%async_computation.7 | async-start | bytes 2752512 | tf_op jit(solution)/shard_map/reduce_scatter | solution.py:39
  45.3 13.7 %copy-start = (bf16[128,4096]{1,0:T(8,128)(2,1)S(1)}, bf16[128,4096]{1,0:T(8,128)(2,1)}, u32[]{:S(2)}) copy-start(bf16[128,4096]{1,0:T(8,128)(2,1)} %all-gather.4.cloned.1.call-done) | copy-start | bytes 3145732
  72.1 83.0 %reduce-scatter.9.cloned.1.call-start = ((), (), s32[]{:S(2)}) async-start(), calls=%async_computation.8 | async-start | bytes 1310720 | tf_op jit(solution)/shard_map/reduce_scatter | solution.py:46
  115.0 40.1 %copy-start.3 = (bf16[2,32,4096]{2,1,0:T(8,128)(2,1)S(1)}, bf16[2,32,4096]{2,1,0:T(8,128)(2,1)}, u32[]{:S(2)}) copy-start(bf16[2,32,4096]{2,1,0:T(8,128)(2,1)} %param.5) | copy-start | bytes 1572868
  115.0 48.8 %copy-start.4 = (f32[1,4096]{1,0:T(1,128)S(1)}, f32[1,4096]{1,0:T(1,128)}, u32[]{:S(2)}) copy-start(f32[1,4096]{1,0:T(1,128)} %param.6) | copy-start | bytes 49156
  127.6 64.0 %all-gather.6.cloned.1.call-start = ((), (), s32[]{:S(2)}) async-start(), calls=%async_computation.9 | async-start | bytes 1310720 | tf_op jit(solution)/shard_map/all_gather | solution.py:35
  156.1 2.5 collective-permute-start
  164.6 82.3 %reduce-scatter.11.cloned.1.call-start = ((), (), s32[]{:S(2)}) async-start(), calls=%async_computation.10 | async-start | bytes 2752512 | tf_op jit(solution)/shard_map/reduce_scatter | solution.py:39
  191.6 13.7 %copy-start.1 = (bf16[128,4096]{1,0:T(8,128)(2,1)S(1)}, bf16[128,4096]{1,0:T(8,128)(2,1)}, u32[]{:S(2)}) copy-start(bf16[128,4096]{1,0:T(8,128)(2,1)} %all-gather.6.cloned.1.call-done) | copy-start | bytes 3145732
  218.4 82.9 %reduce-scatter.13.cloned.1.call-start = ((), (), s32[]{:S(2)}) async-start(), calls=%async_computation.11 | async-start | bytes 1310720 | tf_op jit(solution)/shard_map/reduce_scatter | solution.py:46
  273.8 63.9 %all-gather.8.cloned.1.call-start = ((), (), s32[]{:S(2)}) async-start(), calls=%async_computation.12 | async-start | bytes 1310720 | tf_op jit(solution)/shard_map/all_gather | solution.py:35
  302.3 2.5 collective-permute-start.1
  310.7 82.3 %reduce-scatter.15.cloned.1.call-start = ((), (), s32[]{:S(2)}) async-start(), calls=%async_computation.13 | async-start | bytes 2752512 | tf_op jit(solution)/shard_map/reduce_scatter | solution.py:39
  337.7 13.7 %copy-start.2 = (bf16[128,4096]{1,0:T(8,128)(2,1)S(1)}, bf16[128,4096]{1,0:T(8,128)(2,1)}, u32[]{:S(2)}) copy-start(bf16[128,4096]{1,0:T(8,128)(2,1)} %all-gather.8.cloned.1.call-done) | copy-start | bytes 3145732
  364.5 82.9 %reduce-scatter.17.cloned.1.call-start = ((), (), s32[]{:S(2)}) async-start(), calls=%async_computation.14 | async-start | bytes 1310720 | tf_op jit(solution)/shard_map/reduce_scatter | solution.py:46
Sparse Core Ops, SparseCore 0:
  15.5 29.7 all-gather.3
  72.2 28.3 reduce-scatter.6
  127.7 27.3 reduce-scatter.8
  164.7 26.8 all-gather.5
  218.5 28.3 reduce-scatter.10
  273.9 27.3 reduce-scatter.12
  310.9 26.8 all-gather.7
  364.6 28.3 reduce-scatter.14
  420.1 27.3 reduce-scatter.16
where the time goes:
time: 456 us
  waiting for transfers between devices  254 us (56%)
  matrix products  114 us (25%)
  blocking collectives  54 us (12%)
  other arithmetic  17.9 us (4%)
  between operations  13.4 us (3%)
    reduce_scatter x3, waiting for transfers between devices, on_device(): lax.psum_scatter(pair.astype(jnp.bfloat16), 'row', scatter_dimension=0, t...  85.5 us
    all_gather x3, waiting for transfers between devices, on_device(): normed_rows = lax.all_gather(normed, 'col', axis=0, tiled=True)  83.4 us
    reduce_scatter x3, waiting for transfers between devices, on_device(): lax.psum_scatter(jnp.dot(hidden, down_tile, preferred_element_type=jnp.fl...  82.3 us
    dot_general x3, matrix products, on_device(): up_part = jnp.dot(normed_rows, up_tile, preferred_element_type=jnp.float32)  41.2 us
    all_gather x3, blocking collectives, on_device(): hidden = lax.all_gather(hidden_share, 'row', axis=0, tiled=True)  38.3 us
    dot_general x3, matrix products, on_device(): jnp.dot(hidden, down_tile, preferred_element_type=jnp.float32)  37.7 us
    dot_general x3, matrix products, on_device(): jnp.dot(normed_rows, gate_tile, preferred_element_type=jnp.float32)  34.8 us
    psum x3, blocking collectives, on_device(): sum_sq = lax.psum(jnp.sum(wide_in * wide_in, axis=1), 'row')  15.7 us
  transfers between devices with their start and end apart: 11, of which 11 were waited for; matrix products, arithmetic and copies ran while one was open for 0% of the time, Pallas kernels for 0%

commit v1 on v0

--- a/solution.py
+++ b/solution.py
@@ -32,7 +32,17 @@
         wide = block_in.astype(jnp.float32)
         scale = lax.rsqrt(sum_sq / D + EPS)
         normed = (wide * scale[:, None] * gain[None, :]).astype(jnp.bfloat16)
-        normed_rows = lax.all_gather(normed, "col", axis=0, tiled=True)
+        x = normed
+        ways, here, step = (lax.axis_size("col"), lax.axis_index("col"), x.shape[0])
+        shape = [n * ways if d == 0 else n for d, n in enumerate(x.shape)]
+        normed_rows = lax.dynamic_update_slice_in_dim(
+            jnp.zeros(shape, x.dtype), x, here * step, axis=0
+        )
+        for far in range(1, ways):
+            x = lax.ppermute(x, "col", [(d, (d + 1) % ways) for d in range(ways)])
+            normed_rows = lax.dynamic_update_slice_in_dim(
+                normed_rows, x, (here - far) % ways * step, axis=0
+            )
         gate_part = jnp.dot(normed_rows, gate_tile, preferred_element_type=jnp.float32)
         up_part = jnp.dot(normed_rows, up_tile, preferred_element_type=jnp.float32)
         pair = jnp.concatenate([gate_part, up_part], axis=1)

time: 456 us -> 438 us (0.961)
  waiting for transfers between devices: 254 us -> 241 us
  matrix products: 114 us -> 107 us
    all_gather x3 -> x0, waiting for transfers between devices: 83.4 us -> none  [on_device(): normed_rows = lax.all_gather(normed, 'col', axis=0, tiled=True)]
    ppermute x0 -> x9, waiting for transfers between devices: none -> 74.9 us  [on_device(): x = lax.ppermute(x, 'col', [(d, (d + 1) % ways) for d in range(ways)])]
    dot_general x3, matrix products: 41.2 us -> 34.8 us  [on_device(): up_part = jnp.dot(normed_rows, up_tile, preferred_element_type=jnp.float32)]
  transfers between devices with their start and end apart: 11 -> 17, of which waited for: 11 -> 17; matrix products, arithmetic and copies ran while one was open for 0% -> 0% of each run, Pallas kernels for 0% -> 0%
where the time goes in v1:
time: 438 us
  waiting for transfers between devices  241 us (55%)
  matrix products  107 us (24%)
  blocking collectives  54 us (12%)
  other arithmetic  15.8 us (4%)
  between operations  13.7 us (3%)
  starting transfers between devices  5.22 us (1%)
    reduce_scatter x3, waiting for transfers between devices, on_device(): lax.psum_scatter(jnp.dot(hidden, down_tile, preferred_element_type=jnp.fl...  82.2 us
    reduce_scatter x3, waiting for transfers between devices, on_device(): lax.psum_scatter(pair.astype(jnp.bfloat16), 'row', scatter_dimension=0, t...  81.9 us
    ppermute x9, waiting for transfers between devices, on_device(): x = lax.ppermute(x, 'col', [(d, (d + 1) % ways) for d in range(ways)])  74.9 us
    all_gather x3, blocking collectives, on_device(): hidden = lax.all_gather(hidden_share, 'row', axis=0, tiled=True)  38.3 us
    dot_general x3, matrix products, on_device(): jnp.dot(hidden, down_tile, preferred_element_type=jnp.float32)  37.7 us
    dot_general x3, matrix products, on_device(): up_part = jnp.dot(normed_rows, up_tile, preferred_element_type=jnp.float32)  34.8 us
    dot_general x3, matrix products, on_device(): jnp.dot(normed_rows, gate_tile, preferred_element_type=jnp.float32)  34.8 us
    psum x3, blocking collectives, on_device(): sum_sq = lax.psum(jnp.sum(wide_in * wide_in, axis=1), 'row')  15.7 us
  transfers between devices with their start and end apart: 17, of which 17 were waited for; matrix products, arithmetic and copies ran while one was open for 0% of the time, Pallas kernels for 0%

profile of v1, /device:TPU:0, one launch (start us, length us, event | category | flops | bytes accessed | tf_op | source)
XLA Modules:
  0.0 437.8 jit_solution(18431839533045154283)
XLA Ops:
  6.5 1.1 fusion.56
  7.7 5.9 %psum.21 = f32[32]{0:T(128)S(1)} all-reduce(f32[32]{0:T(128)S(1)} %fusion.56), channel_id=1, replica_groups=mesh['group'=2,'col'=4,'row'=2,'section'=2] {'row'}, use_global_device_ids=true, to_apply=%region_1.2 | all-reduce | flops 32 | bytes 256 | tf_op jit(solution)/shard_map/psum | solution.py:31
  13.6 1.1 constant_dynamic-update-slice_fusion.11
  14.7 2.2 collective-permute-start
  16.9 7.2 %collective-permute-done = bf16[32,4096]{1,0:T(8,128)(2,1)S(1)} collective-permute-done((bf16[32,4096]{1,0:T(8,128)(2,1)S(1)}, bf16[32,4096]{1,0:T(8,128)(2,1)S(1)}, u32[]{:S(2)}, u32[]{:S(2)}) %collective-permute-start) | collective-permute-done | bytes 262176 | tf_op jit(solution)/shard_map/ppermute | solution.py:42
  24.1 8.1 %collective-permute-done.1 = bf16[32,4096]{1,0:T(8,128)(2,1)S(1)} collective-permute-done((bf16[32,4096]{1,0:T(8,128)(2,1)S(1)}, bf16[32,4096]{1,0:T(8,128)(2,1)S(1)}, u32[]{:S(2)}, u32[]{:S(2)}) %collective-permute-start.1) | collective-permute-done | bytes 262176 | tf_op jit(solution)/shard_map/ppermute | solution.py:42
  32.3 8.1 %collective-permute-done.2 = bf16[32,4096]{1,0:T(8,128)(2,1)S(1)} collective-permute-done((bf16[32,4096]{1,0:T(8,128)(2,1)S(1)}, bf16[32,4096]{1,0:T(8,128)(2,1)S(1)}, u32[]{:S(2)}, u32[]{:S(2)}) %collective-permute-start.2) | collective-permute-done | bytes 262176 | tf_op jit(solution)/shard_map/ppermute | solution.py:42
  40.5 11.6 %fusion.18 = bf16[128,3584]{1,0:T(8,128)(2,1)S(1)} fusion(bf16[128,4096]{1,0:T(8,128)(2,1)S(1)} %constant_dynamic-update-slice_fusion.8, bf16[1,4096,3584]{2,1,0:T(8,128)(2,1)} %param.7), kind=kOutput, calls=%fused_computation.18 | convolution fusion | flops 3758555136 | bytes 31326208 | tf_op jit(solution)/shard_map/dot_general | solution.py:46
  52.0 11.6 %fusion.27 = bf16[128,3584]{1,0:T(8,128)(2,1)S(1)} fusion(bf16[128,4096]{1,0:T(8,128)(2,1)S(1)} %constant_dynamic-update-slice_fusion.8, bf16[1,4096,3584]{2,1,0:T(8,128)(2,1)} %param.8), kind=kOutput, calls=%fused_computation.21 | convolution fusion | flops 3758555136 | bytes 31326208 | tf_op jit(solution)/shard_map/dot_general | solution.py:47
  63.6 1.4 pad_maximum_fusion
  65.1 27.4 %reduce-scatter.7.cloned.1.call-done = bf16[64,7168]{1,0:T(8,128)(2,1)} async-done(((bf16[128,7168]{1,0:T(8,128)(2,1)}), bf16[64,7168]{1,0:T(8,128)(2,1)}) %reduce-scatter.7.cloned.1.call-update) | async-done | bytes 917520 | tf_op jit(solution)/shard_map/reduce_scatter | solution.py:49
  92.5 1.3 convert_element_type.75
  93.8 0.2 fusion.47
  94.1 12.8 %all_gather.9 = bf16[128,3584]{1,0:T(8,128)(2,1)S(1)} all-gather(bf16[64,3584]{1,0:T(8,128)(2,1)S(1)} %fusion.47), channel_id=1, replica_groups=mesh['group'=2,'col'=4,'row'=2,'section'=2] {'row'}, dimensions={0}, use_global_device_ids=true | all-gather | bytes 1376256 | tf_op jit(solution)/shard_map/all_gather | solution.py:55
  106.8 12.6 %fusion.36 = bf16[128,4096]{1,0:T(8,128)(2,1)} fusion(bf16[128,3584]{1,0:T(8,128)(2,1)S(1)} %all_gather.9, bf16[1,3584,4096]{2,1,0:T(8,128)(2,1)} %param.9), kind=kOutput, calls=%fused_computation.24 | convolution fusion | flops 3758620672 | bytes 31326208 | tf_op jit(solution)/shard_map/dot_general | solution.py:57
  119.5 27.4 %reduce-scatter.9.cloned.1.call-done = bf16[32,4096]{1,0:T(8,128)(2,1)} async-done(((bf16[128,4096]{1,0:T(8,128)(2,1)}), bf16[32,4096]{1,0:T(8,128)(2,1)}) %reduce-scatter.9.cloned.1.call-update) | async-done | bytes 262160 | tf_op jit(solution)/shard_map/reduce_scatter | solution.py:56
  146.9 1.0 fusion.59
  147.9 1.3 collective-permute-start.3
  149.3 1.1 collective-permute-done.3
  150.6 4.9 %psum.22 = f32[32]{0:T(128)S(1)} all-reduce(f32[32]{0:T(128)S(1)} %get-tuple-element.9), channel_id=1, replica_groups=mesh['group'=2,'col'=4,'row'=2,'section'=2] {'row'}, use_global_device_ids=true, to_apply=%region_5.6 | all-reduce | flops 32 | bytes 256 | tf_op jit(solution)/shard_map/psum | solution.py:31
  155.9 9.2 %collective-permute-done.4 = bf16[32,4096]{1,0:T(8,128)(2,1)S(1)} collective-permute-done((bf16[32,4096]{1,0:T(8,128)(2,1)S(1)}, bf16[32,4096]{1,0:T(8,128)(2,1)S(1)}, u32[]{:S(2)}, u32[]{:S(2)}) %collective-permute-start.4) | collective-permute-done | bytes 262176 | tf_op jit(solution)/shard_map/ppermute | solution.py:42
  165.1 8.3 %collective-permute-done.5 = bf16[32,4096]{1,0:T(8,128)(2,1)S(1)} collective-permute-done((bf16[32,4096]{1,0:T(8,128)(2,1)S(1)}, bf16[32,4096]{1,0:T(8,128)(2,1)S(1)}, u32[]{:S(2)}, u32[]{:S(2)}) %collective-permute-start.5) | collective-permute-done | bytes 262176 | tf_op jit(solution)/shard_map/ppermute | solution.py:42
  173.5 8.1 %collective-permute-done.6 = bf16[32,4096]{1,0:T(8,128)(2,1)S(1)} collective-permute-done((bf16[32,4096]{1,0:T(8,128)(2,1)S(1)}, bf16[32,4096]{1,0:T(8,128)(2,1)S(1)}, u32[]{:S(2)}, u32[]{:S(2)}) %collective-permute-start.6) | collective-permute-done | bytes 262176 | tf_op jit(solution)/shard_map/ppermute | solution.py:42
  181.7 11.6 %fusion.21 = bf16[128,3584]{1,0:T(8,128)(2,1)S(1)} fusion(bf16[128,4096]{1,0:T(8,128)(2,1)S(1)} %constant_dynamic-update-slice_fusion.4, bf16[1,4096,3584]{2,1,0:T(8,128)(2,1)} %param.7), kind=kOutput, calls=%fused_computation.19 | convolution fusion | flops 3758555136 | bytes 31326208 | tf_op jit(solution)/shard_map/dot_general | solution.py:46
  193.3 11.6 %fusion.30 = bf16[128,3584]{1,0:T(8,128)(2,1)S(1)} fusion(bf16[128,4096]{1,0:T(8,128)(2,1)S(1)} %constant_dynamic-update-slice_fusion.4, bf16[1,4096,3584]{2,1,0:T(8,128)(2,1)} %param.8), kind=kOutput, calls=%fused_computation.22 | convolution fusion | flops 3758555136 | bytes 31326208 | tf_op jit(solution)/shard_map/dot_general | solution.py:47
  204.9 1.4 pad_maximum_fusion.1
  206.4 27.3 %reduce-scatter.11.cloned.1.call-done = bf16[64,7168]{1,0:T(8,128)(2,1)} async-done(((bf16[128,7168]{1,0:T(8,128)(2,1)}), bf16[64,7168]{1,0:T(8,128)(2,1)}) %reduce-scatter.11.cloned.1.call-update) | async-done | bytes 917520 | tf_op jit(solution)/shard_map/reduce_scatter | solution.py:49
  233.7 1.3 convert_element_type.82
  235.2 12.8 %all_gather.10 = bf16[128,3584]{1,0:T(8,128)(2,1)S(1)} all-gather(bf16[64,3584]{1,0:T(8,128)(2,1)S(1)} %fusion.46), channel_id=1, replica_groups=mesh['group'=2,'col'=4,'row'=2,'section'=2] {'row'}, dimensions={0}, use_global_device_ids=true | all-gather | bytes 1376256 | tf_op jit(solution)/shard_map/all_gather | solution.py:55
  248.0 12.5 %fusion.39 = bf16[128,4096]{1,0:T(8,128)(2,1)} fusion(bf16[128,3584]{1,0:T(8,128)(2,1)S(1)} %all_gather.10, bf16[1,3584,4096]{2,1,0:T(8,128)(2,1)} %param.9), kind=kOutput, calls=%fused_computation.25 | convolution fusion | flops 3758620672 | bytes 31326208 | tf_op jit(solution)/shard_map/dot_general | solution.py:57
  260.6 27.4 %reduce-scatter.13.cloned.1.call-done = bf16[32,4096]{1,0:T(8,128)(2,1)} async-done(((bf16[128,4096]{1,0:T(8,128)(2,1)}), bf16[32,4096]{1,0:T(8,128)(2,1)}) %reduce-scatter.13.cloned.1.call-update) | async-done | bytes 262160 | tf_op jit(solution)/shard_map/reduce_scatter | solution.py:56
  288.0 1.0 fusion.51
  289.0 1.4 collective-permute-start.7
  290.4 1.1 collective-permute-done.7
  291.7 4.9 %psum.23 = f32[32]{0:T(128)S(1)} all-reduce(f32[32]{0:T(128)S(1)} %fusion.52), channel_id=1, replica_groups=mesh['group'=2,'col'=4,'row'=2,'section'=2] {'row'}, use_global_device_ids=true, to_apply=%region_9.10 | all-reduce | flops 32 | bytes 256 | tf_op jit(solution)/shard_map/psum | solution.py:31
  297.0 9.2 %collective-permute-done.8 = bf16[32,4096]{1,0:T(8,128)(2,1)S(1)} collective-permute-done((bf16[32,4096]{1,0:T(8,128)(2,1)S(1)}, bf16[32,4096]{1,0:T(8,128)(2,1)S(1)}, u32[]{:S(2)}, u32[]{:S(2)}) %collective-permute-start.8) | collective-permute-done | bytes 262176 | tf_op jit(solution)/shard_map/ppermute | solution.py:42
  306.2 8.3 %collective-permute-done.9 = bf16[32,4096]{1,0:T(8,128)(2,1)S(1)} collective-permute-done((bf16[32,4096]{1,0:T(8,128)(2,1)S(1)}, bf16[32,4096]{1,0:T(8,128)(2,1)S(1)}, u32[]{:S(2)}, u32[]{:S(2)}) %collective-permute-start.9) | collective-permute-done | bytes 262176 | tf_op jit(solution)/shard_map/ppermute | solution.py:42
  314.6 8.1 %collective-permute-done.10 = bf16[32,4096]{1,0:T(8,128)(2,1)S(1)} collective-permute-done((bf16[32,4096]{1,0:T(8,128)(2,1)S(1)}, bf16[32,4096]{1,0:T(8,128)(2,1)S(1)}, u32[]{:S(2)}, u32[]{:S(2)}) %collective-permute-start.10) | collective-permute-done | bytes 262176 | tf_op jit(solution)/shard_map/ppermute | solution.py:42
  322.7 11.6 %fusion.24 = bf16[128,3584]{1,0:T(8,128)(2,1)S(1)} fusion(bf16[128,4096]{1,0:T(8,128)(2,1)S(1)} %constant_dynamic-update-slice_fusion, bf16[1,4096,3584]{2,1,0:T(8,128)(2,1)} %param.7), kind=kOutput, calls=%fused_computation.20 | convolution fusion | flops 3758555136 | bytes 31326208 | tf_op jit(solution)/shard_map/dot_general | solution.py:46
  334.3 11.6 %fusion.33 = bf16[128,3584]{1,0:T(8,128)(2,1)S(1)} fusion(bf16[128,4096]{1,0:T(8,128)(2,1)S(1)} %constant_dynamic-update-slice_fusion, bf16[1,4096,3584]{2,1,0:T(8,128)(2,1)} %param.8), kind=kOutput, calls=%fused_computation.23 | convolution fusion | flops 3758555136 | bytes 31326208 | tf_op jit(solution)/shard_map/dot_general | solution.py:47
  345.9 1.4 pad_maximum_fusion.2
  347.5 27.3 %reduce-scatter.15.cloned.1.call-done = bf16[64,7168]{1,0:T(8,128)(2,1)} async-done(((bf16[128,7168]{1,0:T(8,128)(2,1)}), bf16[64,7168]{1,0:T(8,128)(2,1)}) %reduce-scatter.15.cloned.1.call-update) | async-done | bytes 917520 | tf_op jit(solution)/shard_map/reduce_scatter | solution.py:49
  374.7 1.3 convert_element_type.89
  376.3 12.8 %all_gather.11 = bf16[128,3584]{1,0:T(8,128)(2,1)S(1)} all-gather(bf16[64,3584]{1,0:T(8,128)(2,1)S(1)} %fusion.45), channel_id=1, replica_groups=mesh['group'=2,'col'=4,'row'=2,'section'=2] {'row'}, dimensions={0}, use_global_device_ids=true | all-gather | bytes 1376256 | tf_op jit(solution)/shard_map/all_gather | solution.py:55
  389.1 12.5 %fusion.42 = bf16[128,4096]{1,0:T(8,128)(2,1)} fusion(bf16[128,3584]{1,0:T(8,128)(2,1)S(1)} %all_gather.11, bf16[1,3584,4096]{2,1,0:T(8,128)(2,1)} %param.9), kind=kOutput, calls=%fused_computation.26 | convolution fusion | flops 3758620672 | bytes 31326208 | tf_op jit(solution)/shard_map/dot_general | solution.py:57
  401.6 27.4 %reduce-scatter.17.cloned.1.call-done = bf16[32,4096]{1,0:T(8,128)(2,1)} async-done(((bf16[128,4096]{1,0:T(8,128)(2,1)}), bf16[32,4096]{1,0:T(8,128)(2,1)}) %reduce-scatter.17.cloned.1.call-update) | async-done | bytes 262160 | tf_op jit(solution)/shard_map/reduce_scatter | solution.py:56
  429.0 1.0 fusion.60
  430.1 0.9 maximum_select_fusion
  (45 shorter events, 2.1 us)
Async XLA Ops:
  6.5 86.0 %reduce-scatter.7.cloned.1.call-start = ((), (), s32[]{:S(2)}) async-start(), calls=%async_computation.6 | async-start | bytes 2752512 | tf_op jit(solution)/shard_map/reduce_scatter | solution.py:49
  14.7 9.3 %collective-permute-start = (bf16[32,4096]{1,0:T(8,128)(2,1)S(1)}, bf16[32,4096]{1,0:T(8,128)(2,1)S(1)}, u32[]{:S(2)}, u32[]{:S(2)}) collective-permute-start(bf16[32,4096]{1,0:T(8,128)(2,1)S(1)} %get-tuple-element.12), channel_id=1, source_target_pairs={{0,4},{4,8},{8,12},{12,0},{1,5},{5,9},{9,13},{13,1},{2,6},{6,10},{... | collective-permute-start | bytes 786440 | tf_op jit(solution)/shard_map/ppermute | solution.py:42
  24.1 8.2 %collective-permute-start.1 = (bf16[32,4096]{1,0:T(8,128)(2,1)S(1)}, bf16[32,4096]{1,0:T(8,128)(2,1)S(1)}, u32[]{:S(2)}, u32[]{:S(2)}) collective-permute-start(bf16[32,4096]{1,0:T(8,128)(2,1)S(1)} %collective-permute-done), channel_id=1, source_target_pairs={{0,4},{4,8},{8,12},{12,0},{1,5},{5,9},{9,13},{13,1},{2,6},{6,10},{... | collective-permute-start | bytes 786440 | tf_op jit(solution)/shard_map/ppermute | solution.py:42
  32.3 8.2 %collective-permute-start.2 = (bf16[32,4096]{1,0:T(8,128)(2,1)S(1)}, bf16[32,4096]{1,0:T(8,128)(2,1)S(1)}, u32[]{:S(2)}, u32[]{:S(2)}) collective-permute-start(bf16[32,4096]{1,0:T(8,128)(2,1)S(1)} %collective-permute-done.1), channel_id=1, source_target_pairs={{0,4},{4,8},{8,12},{12,0},{1,5},{5,9},{9,13},{13,1},{2,6},{6,10},{... | collective-permute-start | bytes 786440 | tf_op jit(solution)/shard_map/ppermute | solution.py:42
  65.1 81.8 %reduce-scatter.9.cloned.1.call-start = ((), (), s32[]{:S(2)}) async-start(), calls=%async_computation.7 | async-start | bytes 1310720 | tf_op jit(solution)/shard_map/reduce_scatter | solution.py:56
  106.8 40.1 %copy-start = (bf16[2,32,4096]{2,1,0:T(8,128)(2,1)S(1)}, bf16[2,32,4096]{2,1,0:T(8,128)(2,1)}, u32[]{:S(2)}) copy-start(bf16[2,32,4096]{2,1,0:T(8,128)(2,1)} %param.5) | copy-start | bytes 1572868
  119.4 36.3 %copy-start.1 = (f32[1,4096]{1,0:T(1,128)S(1)}, f32[1,4096]{1,0:T(1,128)}, u32[]{:S(2)}) copy-start(f32[1,4096]{1,0:T(1,128)} %param.6) | copy-start | bytes 49156
  119.4 114.2 %reduce-scatter.11.cloned.1.call-start = ((), (), s32[]{:S(2)}) async-start(), calls=%async_computation.8 | async-start | bytes 2752512 | tf_op jit(solution)/shard_map/reduce_scatter | solution.py:49
  147.9 2.5 collective-permute-start.3
  155.8 9.3 %collective-permute-start.4 = (bf16[32,4096]{1,0:T(8,128)(2,1)S(1)}, bf16[32,4096]{1,0:T(8,128)(2,1)S(1)}, u32[]{:S(2)}, u32[]{:S(2)}) collective-permute-start(bf16[32,4096]{1,0:T(8,128)(2,1)S(1)} %get-tuple-element.8), channel_id=1, source_target_pairs={{0,4},{4,8},{8,12},{12,0},{1,5},{5,9},{9,13},{13,1},{2,6},{6,10},{... | collective-permute-start | bytes 786440 | tf_op jit(solution)/shard_map/ppermute | solution.py:42
  165.1 8.4 %collective-permute-start.5 = (bf16[32,4096]{1,0:T(8,128)(2,1)S(1)}, bf16[32,4096]{1,0:T(8,128)(2,1)S(1)}, u32[]{:S(2)}, u32[]{:S(2)}) collective-permute-start(bf16[32,4096]{1,0:T(8,128)(2,1)S(1)} %collective-permute-done.4), channel_id=1, source_target_pairs={{0,4},{4,8},{8,12},{12,0},{1,5},{5,9},{9,13},{13,1},{2,6},{6,10},{... | collective-permute-start | bytes 786440 | tf_op jit(solution)/shard_map/ppermute | solution.py:42
  173.5 8.2 %collective-permute-start.6 = (bf16[32,4096]{1,0:T(8,128)(2,1)S(1)}, bf16[32,4096]{1,0:T(8,128)(2,1)S(1)}, u32[]{:S(2)}, u32[]{:S(2)}) collective-permute-start(bf16[32,4096]{1,0:T(8,128)(2,1)S(1)} %collective-permute-done.5), channel_id=1, source_target_pairs={{0,4},{4,8},{8,12},{12,0},{1,5},{5,9},{9,13},{13,1},{2,6},{6,10},{... | collective-permute-start | bytes 786440 | tf_op jit(solution)/shard_map/ppermute | solution.py:42
  206.3 81.7 %reduce-scatter.13.cloned.1.call-start = ((), (), s32[]{:S(2)}) async-start(), calls=%async_computation.9 | async-start | bytes 1310720 | tf_op jit(solution)/shard_map/reduce_scatter | solution.py:56
  260.6 114.2 %reduce-scatter.15.cloned.1.call-start = ((), (), s32[]{:S(2)}) async-start(), calls=%async_computation.10 | async-start | bytes 2752512 | tf_op jit(solution)/shard_map/reduce_scatter | solution.py:49
  289.0 2.5 collective-permute-start.7
  296.9 9.3 %collective-permute-start.8 = (bf16[32,4096]{1,0:T(8,128)(2,1)S(1)}, bf16[32,4096]{1,0:T(8,128)(2,1)S(1)}, u32[]{:S(2)}, u32[]{:S(2)}) collective-permute-start(bf16[32,4096]{1,0:T(8,128)(2,1)S(1)} %get-tuple-element.6), channel_id=1, source_target_pairs={{0,4},{4,8},{8,12},{12,0},{1,5},{5,9},{9,13},{13,1},{2,6},{6,10},{... | collective-permute-start | bytes 786440 | tf_op jit(solution)/shard_map/ppermute | solution.py:42
  306.2 8.4 %collective-permute-start.9 = (bf16[32,4096]{1,0:T(8,128)(2,1)S(1)}, bf16[32,4096]{1,0:T(8,128)(2,1)S(1)}, u32[]{:S(2)}, u32[]{:S(2)}) collective-permute-start(bf16[32,4096]{1,0:T(8,128)(2,1)S(1)} %collective-permute-done.8), channel_id=1, source_target_pairs={{0,4},{4,8},{8,12},{12,0},{1,5},{5,9},{9,13},{13,1},{2,6},{6,10},{... | collective-permute-start | bytes 786440 | tf_op jit(solution)/shard_map/ppermute | solution.py:42
  314.5 8.2 %collective-permute-start.10 = (bf16[32,4096]{1,0:T(8,128)(2,1)S(1)}, bf16[32,4096]{1,0:T(8,128)(2,1)S(1)}, u32[]{:S(2)}, u32[]{:S(2)}) collective-permute-start(bf16[32,4096]{1,0:T(8,128)(2,1)S(1)} %collective-permute-done.9), channel_id=1, source_target_pairs={{0,4},{4,8},{8,12},{12,0},{1,5},{5,9},{9,13},{13,1},{2,6},{6,10},{... | collective-permute-start | bytes 786440 | tf_op jit(solution)/shard_map/ppermute | solution.py:42
  347.4 81.6 %reduce-scatter.17.cloned.1.call-start = ((), (), s32[]{:S(2)}) async-start(), calls=%async_computation.11 | async-start | bytes 1310720 | tf_op jit(solution)/shard_map/reduce_scatter | solution.py:56
Sparse Core Ops, SparseCore 0:
  65.2 27.2 reduce-scatter.6
  119.6 27.3 reduce-scatter.8
  206.5 27.1 reduce-scatter.10
  260.7 27.2 reduce-scatter.12
  347.5 27.1 reduce-scatter.14
  401.7 27.2 reduce-scatter.16
